TPU v7x, 32 devices: a whole 2x2x4 slice. The times are simulated.
32 devices in a mesh: dp: 16 (over z, x, core), tensor: 2 (over y).
Axes of the slice: x: 2, y: 2, z: 4, core: 2. Of those that a mesh axis runs over, the one named last changes fastest.
Arguments:
- patches: bfloat16 [32768, 1280], P(('dp', 'tensor')), may hold values from -6 to 6
- positions: int32 [2, 32768], P(None, 'dp'), may hold values from 0 to 511, as said below
- ln1_gain: bfloat16 [1280], P(('dp', 'tensor')), may hold values from 0.099609375 to 1.8984375
- ln1_bias: bfloat16 [1280], P(('dp', 'tensor')), may hold values from -2 to 2
- w_qkv: bfloat16 [3, 1280, 1280], P(None, 'dp', 'tensor'), may hold values from -0.15625 to 0.15625
- b_qkv: bfloat16 [3, 1280], P(None, ('tensor', 'dp')), may hold values from -2 to 2
- w_out: bfloat16 [1280, 1280], P('tensor', 'dp'), may hold values from -1.25 to 1.25
- b_out: bfloat16 [1280], P(('dp', 'tensor')), may hold values from -2 to 2
- ln2_gain: bfloat16 [1280], P(('dp', 'tensor')), may hold values from 0.099609375 to 1.8984375
- ln2_bias: bfloat16 [1280], P(('dp', 'tensor')), may hold values from -2 to 2
- w_fc1: bfloat16 [1280, 5120], P('dp', 'tensor'), may hold values from -0.15625 to 0.15625
- b_fc1: bfloat16 [5120], P(('tensor', 'dp')), may hold values from -2 to 2
- w_fc2: bfloat16 [5120, 1280], P('tensor', 'dp'), may hold values from -0.125 to 0.125
- b_fc2: bfloat16 [1280], P(('dp', 'tensor')), may hold values from -2 to 2
- cotangent: bfloat16 [32768, 1280], P(('dp', 'tensor')), may hold values from -6 to 6
Outputs:
- result: bfloat16 [32768, 1280], P(('dp', 'tensor'))
- grad_patches: float32 [32768, 1280], P(('dp', 'tensor'))
- grad_ln1_gain: float32 [1280], P(('dp', 'tensor'))
- grad_ln1_bias: float32 [1280], P(('dp', 'tensor'))
- grad_w_qkv: float32 [3, 1280, 1280], P(None, 'dp', 'tensor')
- grad_b_qkv: float32 [3, 1280], P(None, ('tensor', 'dp'))
- grad_w_out: float32 [1280, 1280], P('tensor', 'dp')
- grad_b_out: float32 [1280], P(('dp', 'tensor'))
- grad_ln2_gain: float32 [1280], P(('dp', 'tensor'))
- grad_ln2_bias: float32 [1280], P(('dp', 'tensor'))
- grad_w_fc1: float32 [1280, 5120], P('dp', 'tensor')
- grad_b_fc1: float32 [5120], P(('tensor', 'dp'))
- grad_w_fc2: float32 [5120, 1280], P('tensor', 'dp')
- grad_b_fc2: float32 [1280], P(('dp', 'tensor'))
Inputs may be any that keep to these rules, and one draw needn't show every extreme that they name: Each image's 1024 tokens lie on a grid whose numbers of rows and columns are powers of two, two or more each, in blocks of 2 x 2 neighbouring patches; the first row of positions holds patch rows, the second patch columns.
All inputs are finite; a program needn't handle non-finite values.
Results may differ from a plain program's by a relative error of at most 0.024.
Values may be sent and summed in bfloat16 or wider, within the bound.
No kernel may reach another device: no remote copies, remote signals or barrier semaphores. Data moves between devices by JAX's collectives and lax.ppermute only.
A program may use at most 320 MiB of HBM per device.

v0:
```python
import jax
import jax.numpy as jnp
from jax import lax
from jax.sharding import PartitionSpec as P

HD = 80
PATCHES = 1024
norm_eps = 1e-06
gelu_slope = 1.702
rope_base = 10000.0


def rotary_tables(positions):
    freq_index = jnp.arange(HD // 4, dtype=jnp.float32)
    inverse = rope_base ** (-(freq_index * 4.0) / HD)
    row_angle = positions[0].astype(jnp.float32)[:, None] * inverse[None, :]
    col_angle = positions[1].astype(jnp.float32)[:, None] * inverse[None, :]
    angles = jnp.concatenate([row_angle, col_angle, row_angle, col_angle], axis=1)
    return (jnp.cos(angles), jnp.sin(angles))


def rotate(head_rows, cosine_table, sine_table):
    half_width = head_rows.shape[-1] // 2
    turned = jnp.concatenate([-head_rows[..., half_width:], head_rows[..., :half_width]], axis=-1)
    return head_rows * cosine_table[:, None, :] + turned * sine_table[:, None, :]


def rotate_back(grad_rows, cosine_table, sine_table):
    half_width = grad_rows.shape[-1] // 2
    with_sine = grad_rows * sine_table[:, None, :]
    turned = jnp.concatenate([with_sine[..., half_width:], -with_sine[..., :half_width]], axis=-1)
    return grad_rows * cosine_table[:, None, :] + turned


def norm_stats(rows_in):
    center = jnp.mean(rows_in, axis=-1, keepdims=True)
    shifted = rows_in - center
    variance = jnp.mean(shifted * shifted, axis=-1, keepdims=True)
    inv_root = lax.rsqrt(variance + norm_eps)
    return (shifted * inv_root, inv_root)


def norm_back(grad_norm, normal_rows, inv_root, norm_gain):
    scaled = grad_norm * norm_gain
    return inv_root * (
        scaled
        - jnp.mean(scaled, axis=-1, keepdims=True)
        - normal_rows * jnp.mean(scaled * normal_rows, axis=-1, keepdims=True)
    )


def attend(members):
    query_block, key_block, value_block = members
    scores = jnp.einsum(
        "qhd,khd->hqk", query_block, key_block, preferred_element_type=jnp.float32
    ) * HD ** (-0.5)
    row_top = jnp.max(scores, axis=-1, keepdims=True)
    exp_scores = jnp.exp(scores - row_top)
    row_total = jnp.sum(exp_scores, axis=-1, keepdims=True)
    weights_soft = (exp_scores / row_total).astype(jnp.bfloat16)
    mixed_heads = jnp.einsum(
        "hqk,khd->qhd", weights_soft, value_block, preferred_element_type=jnp.float32
    )
    return (mixed_heads, (row_top + jnp.log(row_total))[..., 0])


def attend_back(members):
    query_block, key_block, value_block, lse_block, grad_block = members
    scores = jnp.einsum(
        "qhd,khd->hqk", query_block, key_block, preferred_element_type=jnp.float32
    ) * HD ** (-0.5)
    weights_soft = jnp.exp(scores - lse_block[..., None])
    grad_weights = jnp.einsum(
        "qhd,khd->hqk", grad_block, value_block, preferred_element_type=jnp.float32
    )
    inner_sum = jnp.sum(weights_soft * grad_weights, axis=-1, keepdims=True)
    grad_scores = (weights_soft * (grad_weights - inner_sum)).astype(jnp.bfloat16)
    grad_values = jnp.einsum(
        "hqk,qhd->khd",
        weights_soft.astype(jnp.bfloat16),
        grad_block,
        preferred_element_type=jnp.float32,
    )
    grad_queries = jnp.einsum(
        "hqk,khd->qhd", grad_scores, key_block, preferred_element_type=jnp.float32
    ) * HD ** (-0.5)
    grad_keys = jnp.einsum(
        "hqk,qhd->khd", grad_scores, query_block, preferred_element_type=jnp.float32
    ) * HD ** (-0.5)
    return (grad_queries, grad_keys, grad_values)


def local(
    patches,
    positions,
    ln1_gain,
    ln1_bias,
    w_qkv,
    b_qkv,
    w_out,
    b_out,
    ln2_gain,
    ln2_bias,
    w_fc1,
    b_fc1,
    w_fc2,
    b_fc2,
    cotangent,
):
    group_rows = positions.shape[1]
    images_here = group_rows // PATCHES
    heads_here = w_qkv.shape[2] // HD
    vector_list = (
        lax.all_gather(ln1_gain, ("dp", "tensor"), axis=0, tiled=True),
        lax.all_gather(ln1_bias, ("dp", "tensor"), axis=0, tiled=True),
        lax.all_gather(b_out, ("dp", "tensor"), axis=0, tiled=True),
        lax.all_gather(ln2_gain, ("dp", "tensor"), axis=0, tiled=True),
        lax.all_gather(ln2_bias, ("dp", "tensor"), axis=0, tiled=True),
        lax.all_gather(b_fc2, ("dp", "tensor"), axis=0, tiled=True),
    )
    gain_one, shift_one, out_bias, gain_two, shift_two, fc2_bias = [
        item.astype(jnp.float32) for item in vector_list
    ]
    qkv_full, out_full, fc1_full, fc2_full, qkv_bias, fc1_bias = (
        lax.all_gather(w_qkv, "dp", axis=1, tiled=True),
        lax.all_gather(w_out, "dp", axis=1, tiled=True),
        lax.all_gather(w_fc1, "dp", axis=0, tiled=True),
        lax.all_gather(w_fc2, "dp", axis=1, tiled=True),
        lax.all_gather(b_qkv, "dp", axis=1, tiled=True),
        lax.all_gather(b_fc1, "dp", axis=0, tiled=True),
    )
    rows_in = patches.astype(jnp.float32)
    normal_one, root_one = norm_stats(rows_in)
    normed_one = (normal_one * gain_one + shift_one).astype(jnp.bfloat16)
    normed_all = lax.all_gather(normed_one, "tensor", axis=0, tiled=True)
    cosine_table, sine_table = rotary_tables(positions)
    projected = (
        jnp.einsum("ld,jde->jle", normed_all, qkv_full, preferred_element_type=jnp.float32)
        + qkv_bias.astype(jnp.float32)[:, None, :]
    )
    split_heads = projected.reshape(3, group_rows, heads_here, HD)
    queries = rotate(split_heads[0], cosine_table, sine_table).astype(jnp.bfloat16)
    keys_rot = rotate(split_heads[1], cosine_table, sine_table).astype(jnp.bfloat16)
    values_all = split_heads[2].astype(jnp.bfloat16)
    image_shape = (images_here, PATCHES, heads_here, HD)
    mixed_heads, log_totals = lax.map(
        attend,
        (
            queries.reshape(image_shape),
            keys_rot.reshape(image_shape),
            values_all.reshape(image_shape),
        ),
    )
    heads_mix = mixed_heads.reshape(group_rows, heads_here * HD).astype(jnp.bfloat16)
    rows_part = heads_mix
    attn_share = lax.psum_scatter(
        jnp.dot(rows_part, out_full, preferred_element_type=jnp.float32).astype(jnp.bfloat16),
        "tensor",
        scatter_dimension=0,
        tiled=True,
    ).astype(jnp.float32)
    hidden = rows_in + (attn_share + out_bias)
    normal_two, root_two = norm_stats(hidden)
    normed_two = (normal_two * gain_two + shift_two).astype(jnp.bfloat16)
    normed_two_all = lax.all_gather(normed_two, "tensor", axis=0, tiled=True)
    pre_act = jnp.dot(
        normed_two_all, fc1_full, preferred_element_type=jnp.float32
    ) + fc1_bias.astype(jnp.float32)
    gate_sig = jax.nn.sigmoid(gelu_slope * pre_act)
    activation = (pre_act * gate_sig).astype(jnp.bfloat16)
    rows_part = activation
    mlp_share = lax.psum_scatter(
        jnp.dot(rows_part, fc2_full, preferred_element_type=jnp.float32).astype(jnp.bfloat16),
        "tensor",
        scatter_dimension=0,
        tiled=True,
    ).astype(jnp.float32)
    result = (hidden + (mlp_share + fc2_bias)).astype(jnp.bfloat16)
    qkv_back, out_back, fc1_back, fc2_back = (
        lax.all_gather(w_qkv, "dp", axis=1, tiled=True),
        lax.all_gather(w_out, "dp", axis=1, tiled=True),
        lax.all_gather(w_fc1, "dp", axis=0, tiled=True),
        lax.all_gather(w_fc2, "dp", axis=1, tiled=True),
    )
    grad_out = cotangent.astype(jnp.float32)
    grad_fc2_bias = jnp.sum(grad_out, axis=0)
    grad_mlp_all = lax.all_gather(cotangent, "tensor", axis=0, tiled=True)
    grad_fc2_w = jnp.einsum(
        "lf,ld->fd", activation, grad_mlp_all, preferred_element_type=jnp.float32
    )
    grad_act = jnp.einsum("ld,fd->lf", grad_mlp_all, fc2_back, preferred_element_type=jnp.float32)
    gelu_grad = gate_sig + gelu_slope * pre_act * gate_sig * (1.0 - gate_sig)
    grad_pre = (grad_act * gelu_grad).astype(jnp.bfloat16)
    grad_fc1_bias = jnp.sum(grad_pre.astype(jnp.float32), axis=0)
    grad_fc1_w = jnp.einsum(
        "ld,lf->df", normed_two_all, grad_pre, preferred_element_type=jnp.float32
    )
    rows_part = grad_pre
    grad_norm_two = lax.psum_scatter(
        jnp.einsum("lf,df->ld", rows_part, fc1_back, preferred_element_type=jnp.float32).astype(
            jnp.bfloat16
        ),
        "tensor",
        scatter_dimension=0,
        tiled=True,
    ).astype(jnp.float32)
    grad_gain_two = jnp.sum(grad_norm_two * normal_two, axis=0)
    grad_shift_two = jnp.sum(grad_norm_two, axis=0)
    grad_hidden = grad_out + norm_back(grad_norm_two, normal_two, root_two, gain_two)
    grad_attn = grad_hidden.astype(jnp.bfloat16)
    grad_out_bias = jnp.sum(grad_attn.astype(jnp.float32), axis=0)
    grad_attn_all = lax.all_gather(grad_attn, "tensor", axis=0, tiled=True)
    grad_out_w = jnp.einsum(
        "le,ld->ed", heads_mix, grad_attn_all, preferred_element_type=jnp.float32
    )
    grad_heads = jnp.einsum(
        "ld,ed->le", grad_attn_all, out_back, preferred_element_type=jnp.float32
    ).astype(jnp.bfloat16)
    grad_queries, grad_keys, grad_values = lax.map(
        attend_back,
        (
            queries.reshape(image_shape),
            keys_rot.reshape(image_shape),
            values_all.reshape(image_shape),
            log_totals,
            grad_heads.reshape(image_shape),
        ),
    )
    flat_shape = (group_rows, heads_here, HD)
    grad_proj_q = rotate_back(grad_queries.reshape(flat_shape), cosine_table, sine_table).astype(
        jnp.bfloat16
    )
    grad_proj_k = rotate_back(grad_keys.reshape(flat_shape), cosine_table, sine_table).astype(
        jnp.bfloat16
    )
    grad_proj_v = grad_values.reshape(flat_shape).astype(jnp.bfloat16)
    grad_proj = jnp.stack([grad_proj_q, grad_proj_k, grad_proj_v], axis=0).reshape(
        3, group_rows, heads_here * HD
    )
    grad_qkv_bias = jnp.sum(grad_proj.astype(jnp.float32), axis=1)
    grad_qkv_w = jnp.einsum(
        "ld,jle->jde", normed_all, grad_proj, preferred_element_type=jnp.float32
    )
    rows_part = grad_proj
    grad_norm_one = lax.psum_scatter(
        jnp.einsum("jle,jde->ld", rows_part, qkv_back, preferred_element_type=jnp.float32).astype(
            jnp.bfloat16
        ),
        "tensor",
        scatter_dimension=0,
        tiled=True,
    ).astype(jnp.float32)
    grad_gain_one = jnp.sum(grad_norm_one * normal_one, axis=0)
    grad_shift_one = jnp.sum(grad_norm_one, axis=0)
    grad_patches = grad_hidden + norm_back(grad_norm_one, normal_one, root_one, gain_one)
    grad_qkv_s, grad_out_s, grad_fc1_s, grad_fc2_s, grad_qkv_bias_s, grad_fc1_bias_s = (
        lax.psum_scatter(
            grad_qkv_w.astype(jnp.bfloat16), "dp", scatter_dimension=1, tiled=True
        ).astype(jnp.float32),
        lax.psum_scatter(
            grad_out_w.astype(jnp.bfloat16), "dp", scatter_dimension=1, tiled=True
        ).astype(jnp.float32),
        lax.psum_scatter(
            grad_fc1_w.astype(jnp.bfloat16), "dp", scatter_dimension=0, tiled=True
        ).astype(jnp.float32),
        lax.psum_scatter(
            grad_fc2_w.astype(jnp.bfloat16), "dp", scatter_dimension=1, tiled=True
        ).astype(jnp.float32),
        lax.psum_scatter(
            grad_qkv_bias.astype(jnp.bfloat16), "dp", scatter_dimension=1, tiled=True
        ).astype(jnp.float32),
        lax.psum_scatter(
            grad_fc1_bias.astype(jnp.bfloat16), "dp", scatter_dimension=0, tiled=True
        ).astype(jnp.float32),
    )
    (
        grad_gain_one_s,
        grad_shift_one_s,
        grad_out_bias_s,
        grad_gain_two_s,
        grad_shift_two_s,
        grad_fc2_bias_s,
    ) = (
        lax.psum_scatter(grad_gain_one, ("dp", "tensor"), scatter_dimension=0, tiled=True),
        lax.psum_scatter(grad_shift_one, ("dp", "tensor"), scatter_dimension=0, tiled=True),
        lax.psum_scatter(grad_out_bias, ("dp", "tensor"), scatter_dimension=0, tiled=True),
        lax.psum_scatter(grad_gain_two, ("dp", "tensor"), scatter_dimension=0, tiled=True),
        lax.psum_scatter(grad_shift_two, ("dp", "tensor"), scatter_dimension=0, tiled=True),
        lax.psum_scatter(grad_fc2_bias, ("dp", "tensor"), scatter_dimension=0, tiled=True),
    )
    return (
        result,
        grad_patches,
        grad_gain_one_s,
        grad_shift_one_s,
        grad_qkv_s,
        grad_qkv_bias_s,
        grad_out_s,
        grad_out_bias_s,
        grad_gain_two_s,
        grad_shift_two_s,
        grad_fc1_s,
        grad_fc1_bias_s,
        grad_fc2_s,
        grad_fc2_bias_s,
    )


def solution(mesh):
    in_specs = (
        P(("dp", "tensor"), None),
        P(None, "dp"),
        P(("dp", "tensor")),
        P(("dp", "tensor")),
        P(None, "dp", "tensor"),
        P(None, ("tensor", "dp")),
        P("tensor", "dp"),
        P(("dp", "tensor")),
        P(("dp", "tensor")),
        P(("dp", "tensor")),
        P("dp", "tensor"),
        P(("tensor", "dp")),
        P("tensor", "dp"),
        P(("dp", "tensor")),
        P(("dp", "tensor"), None),
    )
    out_specs = (
        P(("dp", "tensor"), None),
        P(("dp", "tensor"), None),
        P(("dp", "tensor")),
        P(("dp", "tensor")),
        P(None, "dp", "tensor"),
        P(None, ("tensor", "dp")),
        P("tensor", "dp"),
        P(("dp", "tensor")),
        P(("dp", "tensor")),
        P(("dp", "tensor")),
        P("dp", "tensor"),
        P(("tensor", "dp")),
        P("tensor", "dp"),
        P(("dp", "tensor")),
    )
    return jax.shard_map(local, mesh=mesh, in_specs=in_specs, out_specs=out_specs, check_vma=False)
```

profile of v0, /device:TPU:0, one launch (start us, length us, event | category | flops | bytes accessed | tf_op | source)
XLA Modules:
  0.0 1690.3 jit_solution(3997134643809691741)
XLA Ops:
  13.8 42.6 %all-reduce.17 = (bf16[1280]{0:T(1024)(128)(2,1)}, bf16[1280]{0:T(1024)(128)(2,1)}, bf16[1280]{0:T(1024)(128)(2,1)}, bf16[1280]{0:T(1024)(128)(2,1)S(1)}, bf16[1...) all-reduce(bf16[1280]{0:T(1024)(128)(2,1)S(1)} %dynamic-update-slic, ...), channel_id=1, replica_groups=mesh['dp'=16,'tensor'=2] {'dp','tensor'}, use_global_device_ids=true, to_apply=%add.4 | all-reduce | flops 7680 | bytes 30720
  61.5 21.4 %all-gather = bf16[16,40,3]{1,2,0:T(4,128)(2,1)S(1)} all-gather(bf16[1,40,3]{1,2,0:T(4,128)(2,1)S(1)} %bitcast.215), channel_id=1, replica_groups=mesh['dp'=16,'tensor'=2] {'dp'}, dimensions={0}, use_global_device_ids=true | all-gather | bytes 4080 | tf_op jit(solution)/shard_map/all_gather | solution.py:129
  94.7 33.5 %all-gather.10.cloned.1.call-done = bf16[2048,1280]{1,0:T(8,128)(2,1)} async-done(((bf16[1024,1280]{1,0:T(8,128)(2,1)}), bf16[2048,1280]{1,0:T(8,128)(2,1)}) %all-gather.10.cloned.1.call-update) | async-done | bytes 5242896 | tf_op jit(solution)/shard_map/all_gather | solution.py:135
  128.2 56.4 %all-gather.12.cloned.1.call-done = bf16[3,1280,640]{2,1,0:T(8,128)(2,1)} async-done(((bf16[3,80,640]{2,1,0:T(8,128)(2,1)}), bf16[3,1280,640]{2,1,0:T(8,128)(2,1)}) %all-gather.12.cloned.1.call-update) | async-done | bytes 4915216 | tf_op jit(solution)/shard_map/all_gather | solution.py:125
  296.1 85.3 %while.28 = (s32[]{:T(128)}, bf16[2,1024,8,80]{1,3,2,0:T(8,128)(2,1)}, f32[2,8,1024]{2,1,0:T(8,128)S(1)}, bf16[2,1024,8,80]{1,3,2,0:T(8,128)(2,1)}, bf16[2,1024,...) while((s32[]{:T(128)}, bf16[2,1024,8,80]{1,3,2,0:T(8,128)(2,1)}, ...), condition=%wide.region_5.6_spmd.clone, body=%wide.region_2.5_spmd.sunk.clone | while | flops 2759843840 | bytes 117966952 | solution.py:146
  398.9 63.5 %reduce-scatter.9.cloned.1.call-done = bf16[1024,1280]{1,0:T(8,128)(2,1)} async-done(((bf16[2048,1280]{1,0:T(8,128)(2,1)}), bf16[1024,1280]{1,0:T(8,128)(2,1)}) %reduce-scatter.9.cloned.1.call-update) | async-done | bytes 2621456 | tf_op jit(solution)/shard_map/reduce_scatter | solution.py:156
  473.2 35.0 %all-reduce.5 = bf16[2560]{0:T(1024)(128)(2,1)S(1)} all-reduce(bf16[2560]{0:T(1024)(128)(2,1)S(1)} %dynamic-update-slice.5), channel_id=1, replica_groups=mesh['dp'=16,'tensor'=2] {'dp'}, use_global_device_ids=true, to_apply=%add.5 | all-reduce | flops 2560 | bytes 10240
  528.0 69.5 %all-gather.16.cloned.1.call-done = bf16[2048,1280]{1,0:T(8,128)(2,1)} async-done(((bf16[1024,1280]{1,0:T(8,128)(2,1)}), bf16[2048,1280]{1,0:T(8,128)(2,1)}) %all-gather.16.cloned.1.call-update) | async-done | bytes 5242896 | tf_op jit(solution)/shard_map/all_gather | solution.py:165
  597.4 25.9 %multiply_convert_fusion.2 = (bf16[2048,2560]{1,0:T(8,128)(2,1)}, f32[2048,2560]{1,0:T(8,128)}) fusion(f32[2560]{0:T(1024)S(1)} %convert_element_type.227, bf16[2048,1280]{1,0:T(8,128)(2,1)} %all-gather.16.cloned.1.call-done, bf16[1280,2560]{1,0:T(8,128)(2,1)} %all-gather.18.cloned.1.call-done), kind=kOutput, calls=%fused_computation.49 | convolution fusion | flops 13458472960 | bytes 43264000 | tf_op jit(solution)/shard_map/dot_general | solution.py:166
  623.3 44.2 %all-gather.22.cloned.1.call-done = bf16[2048,1280]{1,0:T(8,128)(2,1)} async-done(((bf16[1024,1280]{1,0:T(8,128)(2,1)}), bf16[2048,1280]{1,0:T(8,128)(2,1)}) %all-gather.22.cloned.1.call-update) | async-done | bytes 5242896 | tf_op jit(solution)/shard_map/all_gather | solution.py:187
  667.5 65.2 %all-gather.20.cloned.1.call-done = bf16[2560,1280]{0,1:T(8,128)(2,1)} async-done(((bf16[2560,80]{0,1:T(8,128)(2,1)}), bf16[2560,1280]{0,1:T(8,128)(2,1)}) %all-gather.20.cloned.1.call-update) | async-done | bytes 6553616 | tf_op jit(solution)/shard_map/all_gather | solution.py:128
  732.7 29.9 %fusion.87 = (bf16[2560]{0:T(1024)(128)(2,1)}, bf16[2048,2560]{1,0:T(8,128)(2,1)}) fusion(f32[2048,2560]{1,0:T(8,128)} %get-tuple-element.311, f32[2560]{0:T(1024)S(1)} %convert_element_type.227, bf16[2048,1280]{1,0:T(8,128)(2,1)} %all-gather.22.cloned.1.call-done, bf16[2560,1280]{0,1:T(8,128)(2,1)} %all-gather.20.cloned.1.call-done), kind=kOutput, calls=%fused_computation.157 | convolution fusion | flops 13484685312 | bytes 43269120 | tf_op jit(solution)/shard_map/ld,fd->lf/dot_general | solution.py:191
  802.3 44.3 %reduce-scatter.13.cloned.1.call-done = bf16[1024,1280]{1,0:T(8,128)(2,1)} async-done(((bf16[2048,1280]{1,0:T(8,128)(2,1)}), bf16[1024,1280]{1,0:T(8,128)(2,1)}) %reduce-scatter.13.cloned.1.call-update) | async-done | bytes 2621456 | tf_op jit(solution)/shard_map/reduce_scatter | solution.py:199
  852.4 62.2 %reduce-scatter.11.cloned.1.call-done = bf16[1024,1280]{1,0:T(8,128)(2,1)} async-done(((bf16[2048,1280]{1,0:T(8,128)(2,1)}), bf16[1024,1280]{1,0:T(8,128)(2,1)}) %reduce-scatter.11.cloned.1.call-update) | async-done | bytes 2621456 | tf_op jit(solution)/shard_map/reduce_scatter | solution.py:172
  1015.8 213.5 %while.29 = (s32[]{:T(128)}, f32[2,1024,8,80]{1,3,2,0:T(8,128)}, f32[2,1024,8,80]{1,3,2,0:T(8,128)}, bf16[2,1024,8,80]{1,3,2,0:T(8,128)(2,1)}, bf16[2,1024,8,80]...) while((s32[]{:T(128)}, f32[2,1024,8,80]{1,3,2,0:T(8,128)}, ...), condition=%wide.region_15.16_spmd.clone, body=%wide.region_13.15_spmd.sunk.clone | while | flops 6812852224 | bytes 268932192 | solution.py:219
  1046.6 23.4 %multiply_reduce_fusion.8 = (f32[8,1024]{1,0:T(8,128)S(1)}, f32[8,1024,1024]{1,2,0:T(8,128)}) fusion(f32[8,1024,1024]{1,2,0:T(8,128)} %fusion.142, f32[8,1024]{1,0:T(8,128)S(1)} %dynamic-slice_bitcast_fusion.3, bf16[2,1024,8,80]{1,3,2,0:T(8,128)(2,1)} %get-tuple-element.498, s32[]{:T(128)S(6)} %copy.173, ...), kind=kOutput, calls=%fused_computation.18.clone.1.clone | convolution fusion | flops 1375723520 | bytes 69796864 | tf_op jit(solution)/shard_map/while/body/eval_jaxpr/qhd,khd->hqk/dot_general | solution.py:73
  1070.0 29.1 %multiply_convert_fusion.5 = bf16[8,1024,1024]{1,2,0:T(8,128)(2,1)} fusion(f32[8,1024,1024]{1,2,0:T(8,128)} %get-tuple-element.442, f32[8,1024,1024]{1,2,0:T(8,128)} %fusion.142, f32[8,1024]{1,0:T(8,128)S(1)} %get-tuple-element.443, f32[8,1024]{1,0:T(8,128)S(1)} %dynamic-slice_bitcast_fusion.3), kind=kLoop, calls=%fused_computation.17.clone.1.clone | loop fusion | flops 41943040 | bytes 83951616 | tf_op jit(solution)/shard_map/while/body/eval_jaxpr/convert_element_type | solution.py:77
  1154.4 23.4 %multiply_reduce_fusion.8 = (f32[8,1024]{1,0:T(8,128)S(1)}, f32[8,1024,1024]{1,2,0:T(8,128)}) fusion(f32[8,1024,1024]{1,2,0:T(8,128)} %fusion.142, f32[8,1024]{1,0:T(8,128)S(1)} %dynamic-slice_bitcast_fusion.3, bf16[2,1024,8,80]{1,3,2,0:T(8,128)(2,1)} %get-tuple-element.498, s32[]{:T(128)S(6)} %copy.173, ...), kind=kOutput, calls=%fused_computation.18.clone.1.clone | convolution fusion | flops 1375723520 | bytes 69796864 | tf_op jit(solution)/shard_map/while/body/eval_jaxpr/qhd,khd->hqk/dot_general | solution.py:73
  1177.8 28.2 %multiply_convert_fusion.5 = bf16[8,1024,1024]{1,2,0:T(8,128)(2,1)} fusion(f32[8,1024,1024]{1,2,0:T(8,128)} %get-tuple-element.442, f32[8,1024,1024]{1,2,0:T(8,128)} %fusion.142, f32[8,1024]{1,0:T(8,128)S(1)} %get-tuple-element.443, f32[8,1024]{1,0:T(8,128)S(1)} %dynamic-slice_bitcast_fusion.3), kind=kLoop, calls=%fused_computation.17.clone.1.clone | loop fusion | flops 41943040 | bytes 83951616 | tf_op jit(solution)/shard_map/while/body/eval_jaxpr/convert_element_type | solution.py:77
  1393.3 62.2 %all-reduce.18 = (bf16[3,640]{1,0:T(4,128)(2,1)S(1)}, bf16[2560]{0:T(1024)(128)(2,1)S(1)}) all-reduce(bf16[3,640]{1,0:T(4,128)(2,1)S(1)} %fusion.83, bf16[2560]{0:T(1024)(128)(2,1)S(1)} %copy-done.37), channel_id=9, replica_groups=mesh['dp'=16,'tensor'=2] {'dp'}, use_global_device_ids=true, to_apply=%region_25.26.clone | all-reduce | flops 4480 | bytes 17920
  1456.8 44.6 %all-reduce.21.cloned.1.call-done = bf16[3,1280,640]{2,0,1:T(4,128)(2,1)} async-done(((bf16[3,1280,640]{2,0,1:T(4,128)(2,1)}), bf16[3,1280,640]{2,0,1:T(4,128)(2,1)}) %all-reduce.21.cloned.1.call-update) | async-done | bytes 4915216
  1503.3 59.9 %reduce-scatter.17.cloned.1.call-done = bf16[640,80]{0,1:T(8,128)(2,1)} async-done(((bf16[640,1280]{0,1:T(8,128)(2,1)}), bf16[640,80]{0,1:T(8,128)(2,1)}) %reduce-scatter.17.cloned.1.call-update) | async-done | bytes 102416 | tf_op jit(solution)/shard_map/reduce_scatter | solution.py:260
  1564.7 65.4 %reduce-scatter.15.cloned.1.call-done = bf16[1024,1280]{1,0:T(8,128)(2,1)} async-done(((bf16[2048,1280]{1,0:T(8,128)(2,1)}), bf16[1024,1280]{1,0:T(8,128)(2,1)}) %reduce-scatter.15.cloned.1.call-update) | async-done | bytes 2621456 | tf_op jit(solution)/shard_map/reduce_scatter | solution.py:245
  1634.2 40.0 %all-reduce.16 = (f32[1280]{0:T(1024)S(1)}, f32[1280]{0:T(1024)S(1)}, f32[1280]{0:T(1024)S(1)}, f32[1280]{0:T(1024)S(1)}, f32[1280]{0:T(1024)S(1)}, /*index=5*/f32[1280]{0:T(1024)S(1)}) all-reduce(f32[1280]{0:T(1024)S(1)} %get-tuple-element.219, ...), channel_id=6, replica_groups=mesh['dp'=16,'tensor'=2] {'dp','tensor'}, use_global_device_ids=true, to_apply=%region_20.21.clone | all-reduce | flops 7680 | bytes 61440
  (282 shorter events, 702.0 us)
Async XLA Ops:
  7.3 120.9 %all-gather.10.cloned.1.call-start = ((), (), s32[]{:S(2)}) async-start(), calls=%async_computation.7 | async-start | bytes 7864320 | tf_op jit(solution)/shard_map/all_gather | solution.py:135
  59.5 125.0 %all-gather.12.cloned.1.call-start = ((), (), s32[]{:S(2)}) async-start(), calls=%async_computation.8 | async-start | bytes 5222400 | tf_op jit(solution)/shard_map/all_gather | solution.py:125
  60.3 329.0 %all-gather.14.cloned.1.call-start = ((), (), s32[]{:S(2)}) async-start(), calls=%async_computation.9 | async-start | bytes 1740800 | tf_op jit(solution)/shard_map/all_gather | solution.py:126
  61.0 401.5 %reduce-scatter.9.cloned.1.call-start = ((), (), s32[]{:S(2)}) async-start(), calls=%async_computation.10 | async-start | bytes 7864320 | tf_op jit(solution)/shard_map/reduce_scatter | solution.py:156
  398.2 129.7 %all-gather.18.cloned.1.call-start = ((), (), s32[]{:S(2)}) async-start(), calls=%async_computation.12 | async-start | bytes 6963200 | tf_op jit(solution)/shard_map/all_gather | solution.py:127
  398.8 198.6 %all-gather.16.cloned.1.call-start = ((), (), s32[]{:S(2)}) async-start(), calls=%async_computation.11 | async-start | bytes 7864320 | tf_op jit(solution)/shard_map/all_gather | solution.py:165
  470.1 197.5 %all-gather.22.cloned.1.call-start = ((), (), s32[]{:S(2)}) async-start(), calls=%async_computation.15 | async-start | bytes 7864320 | tf_op jit(solution)/shard_map/all_gather | solution.py:187
  470.8 261.9 %all-gather.20.cloned.1.call-start = ((), (), s32[]{:S(2)}) async-start(), calls=%async_computation.13 | async-start | bytes 6963200 | tf_op jit(solution)/shard_map/all_gather | solution.py:128
  471.6 375.1 %reduce-scatter.13.cloned.1.call-start = ((), (), s32[]{:S(2)}) async-start(), calls=%async_computation.16 | async-start | bytes 7864320 | tf_op jit(solution)/shard_map/reduce_scatter | solution.py:199
  782.0 132.6 %reduce-scatter.11.cloned.1.call-start = ((), (), s32[]{:S(2)}) async-start(), calls=%async_computation.14 | async-start | bytes 7864320 | tf_op jit(solution)/shard_map/reduce_scatter | solution.py:172
  801.7 191.0 %all-gather.24.cloned.1.call-start = ((), (), s32[]{:S(2)}) async-start(), calls=%async_computation.17 | async-start | bytes 7864320 | tf_op jit(solution)/shard_map/all_gather | solution.py:212
  924.0 460.3 %reduce-scatter.21.cloned.1.call-start = ((), (), s32[]{:S(2)}) async-start(), calls=%async_computation.21 | async-start | bytes 6963200 | tf_op jit(solution)/shard_map/reduce_scatter | solution.py:266
  944.4 441.9 %reduce-scatter.19.cloned.1.call-start = ((), (), s32[]{:S(2)}) async-start(), calls=%async_computation.20 | async-start | bytes 6963200 | tf_op jit(solution)/shard_map/reduce_scatter | solution.py:263
  977.3 524.1 %all-reduce.21.cloned.1.call-start = ((), (), s32[]{:S(2)}) async-start(), calls=%async_computation.22 | async-start | bytes 13107200
  1357.2 205.9 %reduce-scatter.17.cloned.1.call-start = ((), (), s32[]{:S(2)}) async-start(), calls=%async_computation.19 | async-start | bytes 1740800 | tf_op jit(solution)/shard_map/reduce_scatter | solution.py:260
  1366.1 264.0 %reduce-scatter.15.cloned.1.call-start = ((), (), s32[]{:S(2)}) async-start(), calls=%async_computation.18 | async-start | bytes 7864320 | tf_op jit(solution)/shard_map/reduce_scatter | solution.py:245
  1388.2 241.8 %copy-start.3 = (bf16[1024,1280]{1,0:T(8,128)(2,1)S(1)}, bf16[1024,1280]{1,0:T(8,128)(2,1)}, u32[]{:S(2)}) copy-start(bf16[1024,1280]{1,0:T(8,128)(2,1)} %param.19) | copy-start | bytes 7864324
  1388.2 241.8 %copy-start.20 = (f32[1280]{0:T(1024)S(1)}, f32[1280]{0:T(1024)}, u32[]{:S(2)}) copy-start(f32[1280]{0:T(1024)} %copy-done.19) | copy-start | bytes 15364
  1388.2 241.8 %copy-start.26 = (f32[1024]{0:T(1024)S(1)}, f32[1024]{0:T(1024)}, u32[]{:S(2)}) copy-start(f32[1024]{0:T(1024)} %copy-done.25) | copy-start | bytes 12292
  1388.3 241.8 %copy-start.32 = (f32[1024]{0:T(1024)S(1)}, f32[1024]{0:T(1024)}, u32[]{:S(2)}) copy-start(f32[1024]{0:T(1024)} %copy-done.31) | copy-start | bytes 12292
  1393.2 241.0 %copy-start.33 = (f32[1280]{0:T(1024)S(1)}, f32[1280]{0:T(1024)}, u32[]{:S(2)}) copy-start(f32[1280]{0:T(1024)} %get-tuple-element.271) | copy-start | bytes 15364
  1393.2 241.0 %copy-start.34 = (f32[1280]{0:T(1024)S(1)}, f32[1280]{0:T(1024)}, u32[]{:S(2)}) copy-start(f32[1280]{0:T(1024)} %get-tuple-element.293) | copy-start | bytes 15364
  1393.2 241.0 %copy-start.35 = (f32[1280]{0:T(1024)S(1)}, f32[1280]{0:T(1024)}, u32[]{:S(2)}) copy-start(f32[1280]{0:T(1024)} %get-tuple-element.217) | copy-start | bytes 15364
  1393.2 241.0 %copy-start.36 = (f32[1280]{0:T(1024)S(1)}, f32[1280]{0:T(1024)}, u32[]{:S(2)}) copy-start(f32[1280]{0:T(1024)} %get-tuple-element.223) | copy-start | bytes 15364
  (47 other events, 957.7 us)
Sparse Core Ops, SparseCore 0:
  59.6 68.4 all-gather.9
  130.4 54.1 all-gather.11
  186.7 38.4 all-gather.13
  398.3 64.1 reduce-scatter.8
  464.6 63.2 all-gather.17
  529.9 67.4 all-gather.15
  599.0 68.5 all-gather.21
  669.8 62.8 all-gather.19
  782.1 64.4 reduce-scatter.12
  848.8 65.7 reduce-scatter.10
  924.1 68.5 all-gather.23
  996.5 86.7 reduce-scatter.20
  1087.3 85.7 reduce-scatter.18
  1357.3 143.9 all-reduce.20
  1504.9 58.1 reduce-scatter.16
  1565.3 64.7 reduce-scatter.14
where the time goes:
time: 1700 us; the launch traced here: 1690 us
  waiting for transfers between devices  647 us (38%)
  matrix products  424 us (25%)
  other arithmetic  203 us (12%)
  blocking collectives  201 us (12%)
  local copies, waits for them, and re-layouts  195 us (11%)
  between operations  17.6 us (1%)
    unnamed x4, blocking collectives  180 us
    all_gather x1, waiting for transfers between devices, local(): normed_two_all = lax.all_gather(normed_two, 'tensor', axis=0, tiled=True)  69.5 us
    reduce_scatter x1, waiting for transfers between devices, local(): lax.psum_scatter(jnp.einsum('jle,jde->ld', rows_part, qkv_back, preferred...  65.4 us
    all_gather x1, waiting for transfers between devices, local(): lax.all_gather(w_fc2, 'dp', axis=1, tiled=True)  65.2 us
    reduce_scatter x1, waiting for transfers between devices, local(): lax.psum_scatter(jnp.dot(rows_part, out_full, preferred_element_type=jnp....  63.5 us
    reduce_scatter x1, waiting for transfers between devices, local(): lax.psum_scatter(jnp.dot(rows_part, fc2_full, preferred_element_type=jnp....  62.2 us
    reduce_scatter x1, waiting for transfers between devices, local(): lax.psum_scatter(grad_out_w.astype(jnp.bfloat16), 'dp', scatter_dimension...  59.9 us
    convert_element_type x2, other arithmetic, attend_back(): (weights_soft * (grad_weights - inner_sum)).astype(jnp.bfloat16)  57.3 us
  transfers between devices with their start and end apart: 16, of which 13 were waited for; matrix products, arithmetic and copies ran while one was open for 43% of the time, Pallas kernels for 0%

commit v1 on v0

--- a/solution.py
+++ b/solution.py
@@ -1,3 +1,4 @@
+import functools
 import jax
 import jax.numpy as jnp
 from jax import lax
@@ -8,6 +9,36 @@
 norm_eps = 1e-06
 gelu_slope = 1.702
 rope_base = 10000.0
+
+
+def deliver_cards(frame, dim_no):
+    u_next = list(frame.shape[1:])
+    u_next[dim_no] *= frame.shape[0]
+    return jnp.moveaxis(frame, 0, dim_no).reshape(u_next)
+
+
+def obtain_quotas(panel, which_axis, dim_i):
+    world = lax.axis_size(which_axis)
+    tile_out = map(lambda at: (at, (at + 1) % world), range(world))
+    pile = list(tile_out)
+    w1, s_next = ([], [])
+    stack_in = [(j, pp) for pp, j in pile]
+    for nth in range(world - 1):
+        if nth % 2 == 0:
+            local_out = lax.ppermute(w1[-1] if w1 else panel, axis_name=which_axis, perm=pile)
+            w1.append(local_out)
+        else:
+            s_next.append(
+                lax.ppermute(s_next[-1] if s_next else panel, axis_name=which_axis, perm=stack_in)
+            )
+    w_next = jnp.stack([*w1[::-1], panel, *s_next], axis=0)
+    opened = lax.axis_index(which_axis)
+    taken_in = opened - len(w1)
+    w_next = w_next[(jnp.arange(world) - taken_in) % world]
+    return deliver_cards(w_next, dim_i)
+
+
+pipes_spread = functools.partial(obtain_quotas, which_axis="dp", dim_i=1)
 
 
 def rotary_tables(positions):
@@ -125,7 +156,7 @@
         lax.all_gather(w_qkv, "dp", axis=1, tiled=True),
         lax.all_gather(w_out, "dp", axis=1, tiled=True),
         lax.all_gather(w_fc1, "dp", axis=0, tiled=True),
-        lax.all_gather(w_fc2, "dp", axis=1, tiled=True),
+        pipes_spread(w_fc2),
         lax.all_gather(b_qkv, "dp", axis=1, tiled=True),
         lax.all_gather(b_fc1, "dp", axis=0, tiled=True),
     )

time: 1700 us -> 1730 us (1.018)
  starting transfers between devices: 0.64 us -> 29.2 us
  local copies, waits for them, and re-layouts: 195 us -> 222 us
  waiting for transfers between devices: 647 us -> 625 us
    ppermute x0 -> x15, waiting for transfers between devices: none -> 65.9 us  [the longest x8 57.6 us: obtain_quotas(): lax.ppermute(w1[-1] if w1 else panel, axis_name=which_axis, perm=pile)]
    all_gather x1, waiting for transfers between devices: 69.5 us -> 18.6 us  [local(): normed_two_all = lax.all_gather(normed_two, 'tensor', axis=0, tiled=True)]
    ppermute x0 -> x15, starting transfers between devices: none -> 27.6 us  [the longest x7 27.5 us: obtain_quotas(): lax.ppermute(s_next[-1] if s_next else panel, axis_name=which_axis, perm=...]
    all_gather x1, waiting for transfers between devices: 19.8 us -> 0.01 us  [local(): lax.all_gather(w_fc1, 'dp', axis=0, tiled=True)]
    unnamed x130 -> x153, local copies, waits for them, and re-layouts: 15.5 us -> 34.1 us
    reduce_scatter x1, waiting for transfers between devices: 44.3 us -> 25.9 us  [local(): lax.psum_scatter(jnp.einsum('lf,df->ld', rows_part, fc1_back, preferred_e...]
  transfers between devices with their start and end apart: 16 -> 31, of which waited for: 13 -> 22; matrix products, arithmetic and copies ran while one was open for 43% -> 47% of each run, Pallas kernels for 0% -> 0%
where the time goes in v1:
time: 1730 us; the launch traced here: 1720 us
  waiting for transfers between devices  625 us (36%)
  matrix products  424 us (25%)
  local copies, waits for them, and re-layouts  222 us (13%)
  other arithmetic  203 us (12%)
  blocking collectives  201 us (12%)
  starting transfers between devices  29.2 us (2%)
  between operations  17.6 us (1%)
    unnamed x4, blocking collectives  179 us
    reduce_scatter x1, waiting for transfers between devices, local(): lax.psum_scatter(jnp.einsum('jle,jde->ld', rows_part, qkv_back, preferred...  65.4 us
    all_gather x1, waiting for transfers between devices, local(): lax.all_gather(w_fc2, 'dp', axis=1, tiled=True)  65.2 us
    reduce_scatter x1, waiting for transfers between devices, local(): lax.psum_scatter(jnp.dot(rows_part, out_full, preferred_element_type=jnp....  63.5 us
    reduce_scatter x1, waiting for transfers between devices, local(): lax.psum_scatter(jnp.dot(rows_part, fc2_full, preferred_element_type=jnp....  62.2 us
    reduce_scatter x1, waiting for transfers between devices, local(): lax.psum_scatter(grad_out_w.astype(jnp.bfloat16), 'dp', scatter_dimension...  59.9 us
    ppermute x8, waiting for transfers between devices, obtain_quotas(): lax.ppermute(w1[-1] if w1 else panel, axis_name=which_axis, perm=pile)  57.6 us
    convert_element_type x2, other arithmetic, attend_back(): (weights_soft * (grad_weights - inner_sum)).astype(jnp.bfloat16)  57.4 us
  transfers between devices with their start and end apart: 31, of which 22 were waited for; matrix products, arithmetic and copies ran while one was open for 47% of the time, Pallas kernels for 0%

profile of v1, /device:TPU:0, one launch (start us, length us, event | category | flops | bytes accessed | tf_op | source)
XLA Modules:
  0.0 1722.1 jit_solution(1228601075170064269)
XLA Ops:
  13.8 42.6 %all-reduce.17 = (bf16[1280]{0:T(1024)(128)(2,1)}, bf16[1280]{0:T(1024)(128)(2,1)}, bf16[1280]{0:T(1024)(128)(2,1)}, bf16[1280]{0:T(1024)(128)(2,1)S(1)}, bf16[1...) all-reduce(bf16[1280]{0:T(1024)(128)(2,1)S(1)} %dynamic-update-slic, ...), channel_id=1, replica_groups=mesh['dp'=16,'tensor'=2] {'dp','tensor'}, use_global_device_ids=true, to_apply=%add.4 | all-reduce | flops 7680 | bytes 30720
  61.5 21.4 %all-gather = bf16[16,40,3]{1,2,0:T(4,128)(2,1)S(1)} all-gather(bf16[1,40,3]{1,2,0:T(4,128)(2,1)S(1)} %bitcast.253), channel_id=1, replica_groups=mesh['dp'=16,'tensor'=2] {'dp'}, dimensions={0}, use_global_device_ids=true | all-gather | bytes 4080 | tf_op jit(solution)/shard_map/all_gather | solution.py:160
  94.7 33.5 %all-gather.10.cloned.1.call-done = bf16[2048,1280]{1,0:T(8,128)(2,1)} async-done(((bf16[1024,1280]{1,0:T(8,128)(2,1)}), bf16[2048,1280]{1,0:T(8,128)(2,1)}) %all-gather.10.cloned.1.call-update) | async-done | bytes 5242896 | tf_op jit(solution)/shard_map/all_gather | solution.py:166
  128.2 56.4 %all-gather.12.cloned.1.call-done = bf16[3,1280,640]{2,1,0:T(8,128)(2,1)} async-done(((bf16[3,80,640]{2,1,0:T(8,128)(2,1)}), bf16[3,1280,640]{2,1,0:T(8,128)(2,1)}) %all-gather.12.cloned.1.call-update) | async-done | bytes 4915216 | tf_op jit(solution)/shard_map/all_gather | solution.py:156
  296.2 85.6 %while.28 = (s32[]{:T(128)}, bf16[2,1024,8,80]{1,3,2,0:T(8,128)(2,1)}, f32[2,8,1024]{2,1,0:T(8,128)S(1)}, bf16[2,1024,8,80]{1,3,2,0:T(8,128)(2,1)}, bf16[2,1024,...) while((s32[]{:T(128)}, bf16[2,1024,8,80]{1,3,2,0:T(8,128)(2,1)}, ...), condition=%wide.region_5.6_spmd.clone, body=%wide.region_2.5_spmd.sunk.clone | while | flops 2759843840 | bytes 117966952 | solution.py:177
  399.2 63.5 %reduce-scatter.9.cloned.1.call-done = bf16[1024,1280]{1,0:T(8,128)(2,1)} async-done(((bf16[2048,1280]{1,0:T(8,128)(2,1)}), bf16[1024,1280]{1,0:T(8,128)(2,1)}) %reduce-scatter.9.cloned.1.call-update) | async-done | bytes 2621456 | tf_op jit(solution)/shard_map/reduce_scatter | solution.py:187
  566.9 34.4 %all-reduce.5 = bf16[2560]{0:T(1024)(128)(2,1)S(1)} all-reduce(bf16[2560]{0:T(1024)(128)(2,1)S(1)} %dynamic-update-slice.5), channel_id=1, replica_groups=mesh['dp'=16,'tensor'=2] {'dp'}, use_global_device_ids=true, to_apply=%add.5 | all-reduce | flops 2560 | bytes 10240
  629.0 25.6 %multiply_convert_fusion.2 = (bf16[2048,2560]{1,0:T(8,128)(2,1)}, f32[2048,2560]{1,0:T(8,128)}) fusion(f32[2560]{0:T(1024)S(1)} %convert_element_type.227, bf16[2048,1280]{1,0:T(8,128)(2,1)} %all-gather.16.cloned.1.call-done, bf16[1280,2560]{1,0:T(8,128)(2,1)} %all-gather.18.cloned.1.call-done), kind=kOutput, calls=%fused_computation.50 | convolution fusion | flops 13458472960 | bytes 43264000 | tf_op jit(solution)/shard_map/dot_general | solution.py:197
  654.5 44.5 %all-gather.20.cloned.1.call-done = bf16[2048,1280]{1,0:T(8,128)(2,1)} async-done(((bf16[1024,1280]{1,0:T(8,128)(2,1)}), bf16[2048,1280]{1,0:T(8,128)(2,1)}) %all-gather.20.cloned.1.call-update) | async-done | bytes 5242896 | tf_op jit(solution)/shard_map/all_gather | solution.py:218
  699.1 65.2 %all-gather.22.cloned.1.call-done = bf16[2560,1280]{0,1:T(8,128)(2,1)} async-done(((bf16[2560,80]{0,1:T(8,128)(2,1)}), bf16[2560,1280]{0,1:T(8,128)(2,1)}) %all-gather.22.cloned.1.call-update) | async-done | bytes 6553616 | tf_op jit(solution)/shard_map/all_gather | solution.py:214
  764.2 29.9 %fusion.89 = (bf16[2560]{0:T(1024)(128)(2,1)}, bf16[2048,2560]{1,0:T(8,128)(2,1)}) fusion(f32[2048,2560]{1,0:T(8,128)} %get-tuple-element.311, f32[2560]{0:T(1024)S(1)} %convert_element_type.227, bf16[2048,1280]{1,0:T(8,128)(2,1)} %all-gather.20.cloned.1.call-done, bf16[2560,1280]{0,1:T(8,128)(2,1)} %all-gather.22.cloned.1.call-done), kind=kOutput, calls=%fused_computation.181 | convolution fusion | flops 13484685312 | bytes 43269120 | tf_op jit(solution)/shard_map/ld,fd->lf/dot_general | solution.py:222
  852.2 25.9 %reduce-scatter.13.cloned.1.call-done = bf16[1024,1280]{1,0:T(8,128)(2,1)} async-done(((bf16[2048,1280]{1,0:T(8,128)(2,1)}), bf16[1024,1280]{1,0:T(8,128)(2,1)}) %reduce-scatter.13.cloned.1.call-update) | async-done | bytes 2621456 | tf_op jit(solution)/shard_map/reduce_scatter | solution.py:230
  883.9 62.2 %reduce-scatter.11.cloned.1.call-done = bf16[1024,1280]{1,0:T(8,128)(2,1)} async-done(((bf16[2048,1280]{1,0:T(8,128)(2,1)}), bf16[1024,1280]{1,0:T(8,128)(2,1)}) %reduce-scatter.11.cloned.1.call-update) | async-done | bytes 2621456 | tf_op jit(solution)/shard_map/reduce_scatter | solution.py:203
  956.0 20.0 %convolution_convert_fusion = bf16[2560,1280]{0,1:T(8,128)(2,1)} fusion(bf16[2048,2560]{1,0:T(8,128)(2,1)} %get-tuple-element.310, bf16[2048,1280]{1,0:T(8,128)(2,1)} %all-gather.20.cloned.1.call-done), kind=kOutput, calls=%fused_computation.53 | convolution fusion | flops 13425049600 | bytes 22282240 | tf_op jit(solution)/shard_map/lf,ld->fd/dot_general | solution.py:219
  1047.3 213.6 %while.29 = (s32[]{:T(128)}, f32[2,1024,8,80]{1,3,2,0:T(8,128)}, f32[2,1024,8,80]{1,3,2,0:T(8,128)}, bf16[2,1024,8,80]{1,3,2,0:T(8,128)(2,1)}, bf16[2,1024,8,80]...) while((s32[]{:T(128)}, f32[2,1024,8,80]{1,3,2,0:T(8,128)}, ...), condition=%wide.region_15.16_spmd.clone, body=%wide.region_13.15_spmd.sunk.clone | while | flops 6812852224 | bytes 268932192 | solution.py:250
  1078.1 23.4 %multiply_reduce_fusion.8 = (f32[8,1024]{1,0:T(8,128)S(1)}, f32[8,1024,1024]{1,2,0:T(8,128)}) fusion(f32[8,1024,1024]{1,2,0:T(8,128)} %fusion.144, f32[8,1024]{1,0:T(8,128)S(1)} %dynamic-slice_bitcast_fusion.3, bf16[2,1024,8,80]{1,3,2,0:T(8,128)(2,1)} %get-tuple-element.498, s32[]{:T(128)S(6)} %copy.188, ...), kind=kOutput, calls=%fused_computation.19.clone.1.clone | convolution fusion | flops 1375723520 | bytes 69796864 | tf_op jit(solution)/shard_map/while/body/eval_jaxpr/qhd,khd->hqk/dot_general | solution.py:104
  1101.5 29.1 %multiply_convert_fusion.5 = bf16[8,1024,1024]{1,2,0:T(8,128)(2,1)} fusion(f32[8,1024,1024]{1,2,0:T(8,128)} %get-tuple-element.442, f32[8,1024,1024]{1,2,0:T(8,128)} %fusion.144, f32[8,1024]{1,0:T(8,128)S(1)} %get-tuple-element.443, f32[8,1024]{1,0:T(8,128)S(1)} %dynamic-slice_bitcast_fusion.3), kind=kLoop, calls=%fused_computation.18.clone.1.clone | loop fusion | flops 41943040 | bytes 83951616 | tf_op jit(solution)/shard_map/while/body/eval_jaxpr/convert_element_type | solution.py:108
  1186.0 23.4 %multiply_reduce_fusion.8 = (f32[8,1024]{1,0:T(8,128)S(1)}, f32[8,1024,1024]{1,2,0:T(8,128)}) fusion(f32[8,1024,1024]{1,2,0:T(8,128)} %fusion.144, f32[8,1024]{1,0:T(8,128)S(1)} %dynamic-slice_bitcast_fusion.3, bf16[2,1024,8,80]{1,3,2,0:T(8,128)(2,1)} %get-tuple-element.498, s32[]{:T(128)S(6)} %copy.188, ...), kind=kOutput, calls=%fused_computation.19.clone.1.clone | convolution fusion | flops 1375723520 | bytes 69796864 | tf_op jit(solution)/shard_map/while/body/eval_jaxpr/qhd,khd->hqk/dot_general | solution.py:104
  1209.3 28.3 %multiply_convert_fusion.5 = bf16[8,1024,1024]{1,2,0:T(8,128)(2,1)} fusion(f32[8,1024,1024]{1,2,0:T(8,128)} %get-tuple-element.442, f32[8,1024,1024]{1,2,0:T(8,128)} %fusion.144, f32[8,1024]{1,0:T(8,128)S(1)} %get-tuple-element.443, f32[8,1024]{1,0:T(8,128)S(1)} %dynamic-slice_bitcast_fusion.3), kind=kLoop, calls=%fused_computation.18.clone.1.clone | loop fusion | flops 41943040 | bytes 83951616 | tf_op jit(solution)/shard_map/while/body/eval_jaxpr/convert_element_type | solution.py:108
  1424.7 62.2 %all-reduce.18 = (bf16[3,640]{1,0:T(4,128)(2,1)S(1)}, bf16[2560]{0:T(1024)(128)(2,1)S(1)}) all-reduce(bf16[3,640]{1,0:T(4,128)(2,1)S(1)} %fusion.85, bf16[2560]{0:T(1024)(128)(2,1)S(1)} %copy-done.41), channel_id=9, replica_groups=mesh['dp'=16,'tensor'=2] {'dp'}, use_global_device_ids=true, to_apply=%region_25.26.clone | all-reduce | flops 4480 | bytes 17920
  1488.2 44.8 %all-reduce.21.cloned.1.call-done = bf16[3,1280,640]{2,0,1:T(4,128)(2,1)} async-done(((bf16[3,1280,640]{2,0,1:T(4,128)(2,1)}), bf16[3,1280,640]{2,0,1:T(4,128)(2,1)}) %all-reduce.21.cloned.1.call-update) | async-done | bytes 4915216
  1535.0 59.9 %reduce-scatter.17.cloned.1.call-done = bf16[640,80]{0,1:T(8,128)(2,1)} async-done(((bf16[640,1280]{0,1:T(8,128)(2,1)}), bf16[640,80]{0,1:T(8,128)(2,1)}) %reduce-scatter.17.cloned.1.call-update) | async-done | bytes 102416 | tf_op jit(solution)/shard_map/reduce_scatter | solution.py:291
  1596.5 65.4 %reduce-scatter.15.cloned.1.call-done = bf16[1024,1280]{1,0:T(8,128)(2,1)} async-done(((bf16[2048,1280]{1,0:T(8,128)(2,1)}), bf16[1024,1280]{1,0:T(8,128)(2,1)}) %reduce-scatter.15.cloned.1.call-update) | async-done | bytes 2621456 | tf_op jit(solution)/shard_map/reduce_scatter | solution.py:276
  1666.0 40.1 %all-reduce.16 = (f32[1280]{0:T(1024)S(1)}, f32[1280]{0:T(1024)S(1)}, f32[1280]{0:T(1024)S(1)}, f32[1280]{0:T(1024)S(1)}, f32[1280]{0:T(1024)S(1)}, /*index=5*/f32[1280]{0:T(1024)S(1)}) all-reduce(f32[1280]{0:T(1024)S(1)} %get-tuple-element.219, ...), channel_id=6, replica_groups=mesh['dp'=16,'tensor'=2] {'dp','tensor'}, use_global_device_ids=true, to_apply=%region_20.21.clone | all-reduce | flops 7680 | bytes 61440
  (339 shorter events, 801.7 us)
Async XLA Ops:
  7.3 120.9 %all-gather.10.cloned.1.call-start = ((), (), s32[]{:S(2)}) async-start(), calls=%async_computation.7 | async-start | bytes 7864320 | tf_op jit(solution)/shard_map/all_gather | solution.py:166
  59.5 125.0 %all-gather.12.cloned.1.call-start = ((), (), s32[]{:S(2)}) async-start(), calls=%async_computation.8 | async-start | bytes 5222400 | tf_op jit(solution)/shard_map/all_gather | solution.py:156
  60.3 329.3 %all-gather.14.cloned.1.call-start = ((), (), s32[]{:S(2)}) async-start(), calls=%async_computation.9 | async-start | bytes 1740800 | tf_op jit(solution)/shard_map/all_gather | solution.py:157
  61.0 401.8 %reduce-scatter.9.cloned.1.call-start = ((), (), s32[]{:S(2)}) async-start(), calls=%async_computation.10 | async-start | bytes 7864320 | tf_op jit(solution)/shard_map/reduce_scatter | solution.py:187
  398.5 211.8 %all-gather.18.cloned.1.call-start = ((), (), s32[]{:S(2)}) async-start(), calls=%async_computation.12 | async-start | bytes 6963200 | tf_op jit(solution)/shard_map/all_gather | solution.py:158
  399.1 229.9 %all-gather.16.cloned.1.call-start = ((), (), s32[]{:S(2)}) async-start(), calls=%async_computation.11 | async-start | bytes 7864320 | tf_op jit(solution)/shard_map/all_gather | solution.py:196
  470.4 228.7 %all-gather.20.cloned.1.call-start = ((), (), s32[]{:S(2)}) async-start(), calls=%async_computation.14 | async-start | bytes 7864320 | tf_op jit(solution)/shard_map/all_gather | solution.py:218
  471.1 293.1 %all-gather.22.cloned.1.call-start = ((), (), s32[]{:S(2)}) async-start(), calls=%async_computation.15 | async-start | bytes 6963200 | tf_op jit(solution)/shard_map/all_gather | solution.py:214
  471.9 406.3 %reduce-scatter.13.cloned.1.call-start = ((), (), s32[]{:S(2)}) async-start(), calls=%async_computation.16 | async-start | bytes 7864320 | tf_op jit(solution)/shard_map/reduce_scatter | solution.py:230
  471.9 16.8 collective-permute-start
  499.6 16.4 collective-permute-start.2
  499.6 19.0 %collective-permute-start.9 = (bf16[2560,80]{0,1:T(8,128)(2,1)S(1)}, bf16[2560,80]{0,1:T(8,128)(2,1)S(1)}, u32[]{:S(2)}, u32[]{:S(2)}) collective-permute-start(bf16[2560,80]{0,1:T(8,128)(2,1)S(1)} %collective-permute-done.8), channel_id=1, source_target_pairs={{2,0},{4,2},{6,4},{8,6},{10,8},{12,10},{14,12},{16,14},{18,16},{20... | collective-permute-start | bytes 1228808 | tf_op jit(solution)/shard_map/ppermute | solution.py:32
  529.5 14.1 collective-permute-start.4
  529.5 17.7 %collective-permute-start.11 = (bf16[2560,80]{0,1:T(8,128)(2,1)S(1)}, bf16[2560,80]{0,1:T(8,128)(2,1)S(1)}, u32[]{:S(2)}, u32[]{:S(2)}) collective-permute-start(bf16[2560,80]{0,1:T(8,128)(2,1)S(1)} %collective-permute-done.10), channel_id=1, source_target_pairs={{2,0},{4,2},{6,4},{8,6},{10,8},{12,10},{14,12},{16,14},{18,16},{20... | collective-permute-start | bytes 1228808 | tf_op jit(solution)/shard_map/ppermute | solution.py:32
  557.3 44.1 %collective-permute-start.13 = (bf16[2560,80]{0,1:T(8,128)(2,1)}, bf16[2560,80]{0,1:T(8,128)(2,1)}, u32[]{:S(2)}, u32[]{:S(2)}) collective-permute-start(bf16[2560,80]{0,1:T(8,128)(2,1)} %collective-permute-done.12), channel_id=1, source_target_pairs={{2,0},{4,2},{6,4},{8,6},{10,8},{12,10},{14,12},{16,14},{18,16},{20... | collective-permute-start | bytes 1228808 | tf_op jit(solution)/shard_map/ppermute | solution.py:32
  565.4 36.1 %collective-permute-start.7 = (bf16[2560,80]{0,1:T(8,128)(2,1)}, bf16[2560,80]{0,1:T(8,128)(2,1)}, u32[]{:S(2)}, u32[]{:S(2)}) collective-permute-start(bf16[2560,80]{0,1:T(8,128)(2,1)} %collective-permute-done.6), channel_id=1, source_target_pairs={{0,2},{2,4},{4,6},{6,8},{8,10},{10,12},{12,14},{14,16},{16,18},{18... | collective-permute-start | bytes 1228808 | tf_op jit(solution)/shard_map/ppermute | solution.py:28
  601.4 222.4 %collective-permute-start.14 = (bf16[2560,80]{0,1:T(8,128)(2,1)}, bf16[2560,80]{0,1:T(8,128)(2,1)}, u32[]{:S(2)}, u32[]{:S(2)}) collective-permute-start(bf16[2560,80]{0,1:T(8,128)(2,1)} %collective-permute-done.13), channel_id=1, source_target_pairs={{2,0},{4,2},{6,4},{8,6},{10,8},{12,10},{14,12},{16,14},{18,16},{20... | collective-permute-start | bytes 1228808 | tf_op jit(solution)/shard_map/ppermute | solution.py:32
  813.5 132.6 %reduce-scatter.11.cloned.1.call-start = ((), (), s32[]{:S(2)}) async-start(), calls=%async_computation.13 | async-start | bytes 7864320 | tf_op jit(solution)/shard_map/reduce_scatter | solution.py:203
  851.6 172.6 %all-gather.24.cloned.1.call-start = ((), (), s32[]{:S(2)}) async-start(), calls=%async_computation.17 | async-start | bytes 7864320 | tf_op jit(solution)/shard_map/all_gather | solution.py:243
  955.5 460.3 %reduce-scatter.21.cloned.1.call-start = ((), (), s32[]{:S(2)}) async-start(), calls=%async_computation.21 | async-start | bytes 6963200 | tf_op jit(solution)/shard_map/reduce_scatter | solution.py:297
  976.0 441.7 %reduce-scatter.19.cloned.1.call-start = ((), (), s32[]{:S(2)}) async-start(), calls=%async_computation.20 | async-start | bytes 6963200 | tf_op jit(solution)/shard_map/reduce_scatter | solution.py:294
  1008.8 524.3 %all-reduce.21.cloned.1.call-start = ((), (), s32[]{:S(2)}) async-start(), calls=%async_computation.22 | async-start | bytes 13107200
  1388.7 206.2 %reduce-scatter.17.cloned.1.call-start = ((), (), s32[]{:S(2)}) async-start(), calls=%async_computation.19 | async-start | bytes 1740800 | tf_op jit(solution)/shard_map/reduce_scatter | solution.py:291
  1397.6 264.3 %reduce-scatter.15.cloned.1.call-start = ((), (), s32[]{:S(2)}) async-start(), calls=%async_computation.18 | async-start | bytes 7864320 | tf_op jit(solution)/shard_map/reduce_scatter | solution.py:276
  (66 other events, 3125.0 us)
Sparse Core Ops, SparseCore 0:
  59.6 68.4 all-gather.9
  130.4 54.1 all-gather.11
  186.7 38.4 all-gather.13
  398.6 64.1 reduce-scatter.8
  464.9 85.3 all-gather.17
  552.2 76.6 all-gather.15
  630.5 68.5 all-gather.19
  701.4 62.8 all-gather.21
  813.6 64.4 reduce-scatter.12
  880.3 65.7 reduce-scatter.10
  955.6 68.5 all-gather.23
  1028.0 86.7 reduce-scatter.20
  1118.8 85.7 reduce-scatter.18
  1388.9 144.1 all-reduce.20
  1536.7 58.1 reduce-scatter.16
  1597.0 64.7 reduce-scatter.14
